TPU v7x, 512 devices: a whole 4x8x8 slice. The times are simulated.
512 devices in a mesh: dp: 32 (over x_lo, z, core), ctx: 16 (over y, x_hi).
Axes of the slice: x: 4 (x_hi: 2, x_lo: 2; x = x_hi * 2 + x_lo), y: 8, z: 8, core: 2. Of those that a mesh axis runs over, the one named last changes fastest.
Arguments:
- layer_input: bfloat16 [32, 2048, 8192], P('dp', 'ctx'), may hold values from -6 to 6
- queries: bfloat16 [32, 2048, 1024], P('dp', 'ctx'), may hold values from -68 to 68
- key_rows: bfloat16 [32, 2048, 128], P('dp', 'ctx'), may hold values from -4 to 4
- value_rows: bfloat16 [32, 2048, 128], P('dp', 'ctx'), may hold values from -5 to 5
- grad_output: bfloat16 [32, 2048, 1024], P('dp', 'ctx'), may hold values from -12 to 12
- segments: int32 [32, 2048], P('dp'), may hold values from 0 to 2, never falling along the last dimension, each value on 1 to 1024 neighbouring positions
- lengths: int32 [32], P('dp'), may hold values from 1024 to 2048, as said below
Outputs:
- grad_queries: bfloat16 [32, 2048, 1024], P('dp', 'ctx')
- grad_weights: bfloat16 [8192, 256], P(('dp', 'ctx'))
Inputs may be any that keep to these rules, and one draw needn't show every extreme that they name: `lengths`: some rollout has all 2048 positions live.
All inputs are finite; a program needn't handle non-finite values.
Results may differ from a plain program's by a relative error of at most 0.0057.
Values may be sent and summed in bfloat16 or wider, within the bound.
No kernel may reach another device: no remote copies, remote signals or barrier semaphores. Data moves between devices by JAX's collectives and lax.ppermute only.
A program may use at most 64 MiB of HBM per device.

v0:
```python
import math

import jax
import jax.numpy as jnp
from jax import lax
from jax.experimental import pallas as pl
from jax.experimental.pallas import tpu as pltpu
from jax.sharding import Mesh, PartitionSpec as P


NAMES = ("x_lo", "z", "core", "y", "x_hi")
DP = NAMES[:3]
CTX = NAMES[3:]
BACK = 4
NEG = -1e30
BF16 = jnp.bfloat16
F32 = jnp.float32


def contract(a, b, dim_a, dim_b):
    return lax.dot_general(
        a, b, (((dim_a,), (dim_b,)), ((), ())), preferred_element_type=F32
    )


def attention_kernel(scale, group, window, at_ref, length_ref, seg_ref, q_ref, up_ref, *refs):
    pairs = [r[...] for r in refs[: BACK + 1]]
    gq_ref, own_ref = refs[BACK + 1], refs[BACK + 2]
    out_refs = refs[BACK + 3 : 2 * BACK + 3]
    ds_ref, p_ref, bias_ref = refs[2 * BACK + 3 :]
    hd = pairs[0].shape[1] // 2
    rows = q_ref.shape[0]
    keys = jnp.concatenate([p[:, :hd] for p in pairs], axis=0)
    values = jnp.concatenate([p[:, hd:] for p in pairs], axis=0)
    first = pl.multiple_of(at_ref[1], rows)
    place = first + lax.broadcasted_iota(jnp.int32, (1, rows), 1)
    own_seg = seg_ref[:, pl.ds(first, rows)]
    seg_row = seg_ref[...]
    lower = [jnp.sum((seg_row < n).astype(jnp.int32), axis=1, keepdims=True) for n in (1, 2)]
    start = jnp.where(own_seg == 0, 0, jnp.where(own_seg == 1, lower[0], lower[1]))
    low = jnp.maximum(start, place - (window - 1))
    high = jnp.minimum(place, length_ref[0])
    live = (place < length_ref[0]).astype(F32)
    live = jnp.concatenate([live] * 2, axis=1)
    size = pairs[0].shape[0]
    for k in range(BACK + 1):
        key_place = at_ref[0] - k * size + lax.broadcasted_iota(jnp.int32, (size, rows), 0)
        allowed = ((key_place >= low) & (key_place < high)) | (key_place == place)
        bias_ref[k * size : (k + 1) * size, :] = jnp.where(allowed, 0.0, NEG)
    keys_turned = keys.T
    for h in range(0, group, 2):
        heads = [slice(g * hd, (g + 1) * hd) for g in (h, h + 1)]
        cols = slice(h * rows, (h + 2) * rows)
        q_two = jnp.concatenate([q_ref[:, s] for s in heads], axis=0)
        up_two = jnp.concatenate([up_ref[:, s] for s in heads], axis=0)
        bias = jnp.concatenate([bias_ref[...]] * 2, axis=1)
        scores = contract(keys, q_two, 1, 1) * scale + bias
        top = jnp.max(scores, axis=0, keepdims=True)
        raised = jnp.exp(scores - top)
        probs = raised * (live / jnp.sum(raised, axis=0, keepdims=True))
        dprobs = contract(values, up_two, 1, 1)
        rowdot = jnp.sum(probs * dprobs, axis=0, keepdims=True)
        dscores = (probs * (dprobs - rowdot)).astype(BF16)
        ds_ref[:, cols] = dscores
        p_ref[:, cols] = probs.astype(BF16)
        grad_q = (contract(keys_turned, dscores, 1, 0).T * scale).astype(BF16)
        for n, s in enumerate(heads):
            gq_ref[:, s] = grad_q[n * rows : (n + 1) * rows]
    q_all = jnp.concatenate([q_ref[:, g * hd : (g + 1) * hd] for g in range(group)], axis=0)
    up_all = jnp.concatenate([up_ref[:, g * hd : (g + 1) * hd] for g in range(group)], axis=0)
    grad_k = contract(ds_ref[...], q_all, 1, 0) * scale
    grad_v = contract(p_ref[...], up_all, 1, 0)
    own_ref[:, :hd] = grad_k[:size]
    own_ref[:, hd:] = grad_v[:size]
    for k, ref in enumerate(out_refs, 1):
        ref[:, :hd] = grad_k[k * size : (k + 1) * size].astype(BF16)
        ref[:, hd:] = grad_v[k * size : (k + 1) * size].astype(BF16)


def attention(at, lengths, segments, queries, upstream, pairs, scale, window):
    rows, wide = queries.shape
    size, two = pairs[0].shape
    group = wide // (two // 2)
    total = size * (BACK + 1)

    def kernel(*refs):
        attention_kernel(scale, group, window, *refs)

    return pl.pallas_call(
        kernel,
        out_shape=[jax.ShapeDtypeStruct((rows, wide), BF16)]
        + [jax.ShapeDtypeStruct((size, two), F32)]
        + [jax.ShapeDtypeStruct((size, two), BF16)] * BACK,
        in_specs=[pl.BlockSpec(memory_space=pltpu.SMEM)] * 2
        + [pl.BlockSpec(memory_space=pltpu.VMEM)] * (4 + BACK),
        scratch_shapes=[pltpu.VMEM((total, rows * group), BF16)] * 2
        + [pltpu.VMEM((total, rows), F32)],
        cost_estimate=pl.CostEstimate(
            flops=5 * 2 * total * rows * wide,
            bytes_accessed=4 * total * two,
            transcendentals=total * rows * group,
        ),
        compiler_params=pltpu.CompilerParams(vmem_limit_bytes=32 << 20),
        name="window_attention",
    )(at, lengths, segments, queries, upstream, *pairs)


def weights_kernel(at_ref, *refs):
    inputs, grads, out_ref = refs[:4], refs[4:7], refs[7]
    rows = grads[0].shape[0] // 2
    total = None
    for n, x in enumerate(inputs):
        at = pl.ds(pl.multiple_of(at_ref[n % 2] * rows, rows), rows)
        if n < 2:
            parts = [grads[0][at, :], grads[1][at, :]]
        else:
            parts = [grads[2][0, at, :], grads[2][1, at, :]]
        term = contract(x[...], jnp.concatenate(parts, axis=0), 1, 0)
        total = term if total is None else total + term
    out_ref[...] = total.astype(BF16)


def weight_partials(at, inputs, grads, steps):
    count, deep = inputs[0].shape
    tall = count // steps
    wide = grads[0].shape[1]
    return pl.pallas_call(
        weights_kernel,
        out_shape=jax.ShapeDtypeStruct((count, wide), BF16),
        grid=(steps,),
        in_specs=[pl.BlockSpec(memory_space=pltpu.SMEM)]
        + [pl.BlockSpec((tall, deep), lambda j: (j, 0))] * 4
        + [pl.BlockSpec(grads[0].shape, lambda j: (0, 0))] * 2
        + [pl.BlockSpec(grads[2].shape, lambda j: (0, 0, 0))],
        out_specs=pl.BlockSpec((tall, wide), lambda j: (j, 0)),
        cost_estimate=pl.CostEstimate(
            flops=2 * count * wide * deep * 4,
            bytes_accessed=2 * deep * 4 * (count + wide),
            transcendentals=0,
        ),
        compiler_params=pltpu.CompilerParams(vmem_limit_bytes=16 << 20),
        name="weight_partials",
    )(at, *inputs, *grads)


def y_shift(x, by):
    count = lax.axis_size("y")
    return lax.ppermute(x, "y", [(i, i + by) for i in range(count) if 0 <= i + by < count])


def flipped(x, axis):
    return lax.ppermute(x, axis, [(0, 1), (1, 0)])


def x_swap(x, flip_low, flip_high):
    pairs = [(i, i ^ (2 * flip_low + flip_high)) for i in range(4)]
    return lax.ppermute(x, ("x_lo", "x_hi"), pairs)


STEPS = range(1, BACK + 1)


def step(layer_input, queries, key_rows, value_rows, grad_output, segments, lengths):
    y_count = lax.axis_size("y")
    z_count = lax.axis_size("z")
    dp_count = 4 * z_count
    x_lo = lax.axis_index("x_lo")
    core = lax.axis_index("core")
    y_at = lax.axis_index("y")
    x_hi = lax.axis_index("x_hi")
    rows = layer_input.shape[1]
    width_all = layer_input.shape[2]
    head_size = key_rows.shape[2]
    pair_rows = 2 * rows
    scale = 1.0 / math.sqrt(head_size)

    local_pair = jnp.concatenate([key_rows[0], value_rows[0]], axis=1)
    other_pair = flipped(local_pair, "x_hi")
    both = jnp.concatenate(
        [
            jnp.where(x_hi == 0, local_pair, other_pair),
            jnp.where(x_hi == 0, other_pair, local_pair),
        ],
        axis=0,
    )
    pairs = [both]
    for k in range(1, BACK):
        pairs.append(y_shift(both, k))
    half = BACK // 2
    if y_count == 2 * BACK:
        first = [(i, (i - half) % y_count) for i in range(BACK)]
        second = [((i - half) % y_count, i + BACK) for i in range(BACK)]
        passing = lax.ppermute(both, "y", first)
        pairs.append(lax.ppermute(passing, "y", second))
    else:
        pairs.append(y_shift(both, BACK))

    fine = width_all // (2 * z_count * 2 * y_count * 2)
    count = z_count * y_count * fine
    turned = layer_input[0].T
    columns = turned.reshape(2, z_count, 2, y_count, 2, fine, rows)
    to_core = lax.dynamic_slice(
        columns, (0, 0, 1 - core, 0, 0, 0, 0), (2, z_count, 1, y_count, 2, fine, rows)
    )
    from_core = flipped(to_core.reshape(4 * count, rows), "core")
    core_columns = from_core.reshape(2, z_count, y_count, 2, fine, rows)

    def piece(flip_low, flip_high):
        low_to, high_to = x_lo ^ flip_low, x_hi ^ flip_high
        mine = lax.dynamic_slice(
            columns,
            (low_to, 0, core, 0, high_to, 0, 0),
            (1, z_count, 1, y_count, 1, fine, rows),
        )
        theirs = lax.dynamic_slice(
            core_columns, (low_to, 0, 0, high_to, 0, 0), (1, z_count, y_count, 1, fine, rows)
        )
        return jnp.concatenate([mine.reshape(count, rows), theirs.reshape(count, rows)], axis=1)

    inputs = [piece(0, 0)]
    for flips in ((0, 1), (1, 0), (1, 1)):
        inputs.append(x_swap(piece(*flips), *flips))

    base = y_at * pair_rows
    where = jnp.stack([base, base + x_hi * rows]).astype(jnp.int32)
    grad_q, own, *low = attention(
        where, lengths, segments, queries[0], grad_output[0], pairs, scale, 8 * rows
    )

    total = own
    for k in STEPS:
        came = y_shift(low[k - 1], -k)
        total = total + came.astype(F32)
    came = flipped(total.astype(BF16), "x_hi")
    grad_kv = (total + came.astype(F32)).astype(BF16)
    core_grad = flipped(grad_kv, "core")
    x_grads = flipped(jnp.stack([grad_kv, core_grad]), "x_lo")
    at = jnp.stack([x_hi, 1 - x_hi]).astype(jnp.int32)
    partial_value = weight_partials(at, inputs, [grad_kv, core_grad, x_grads], 4)

    peers = z_count * y_count
    pieces = partial_value.reshape(peers, fine, 2 * head_size)
    moved = lax.all_to_all(pieces, ("z", "y"), split_axis=0, concat_axis=0, tiled=True)
    summed = jnp.sum(moved.astype(F32), axis=0)
    grad_weights = (summed / dp_count).astype(BF16)
    return (grad_q[None], grad_weights)


def solution(mesh):
    devices = mesh.devices
    dp_count, ctx_count = devices.shape
    fine = Mesh(devices.reshape(2, dp_count // 4, 2, ctx_count // 2, 2), NAMES)
    return jax.shard_map(
        step,
        mesh=fine,
        in_specs=(
            P(DP, CTX, None),
            P(DP, CTX, None),
            P(DP, CTX, None),
            P(DP, CTX, None),
            P(DP, CTX, None),
            P(DP, None),
            P(DP),
        ),
        out_specs=(P(DP, CTX, None), P(NAMES, None)),
        check_vma=False,
    )
```

profile of v0, /device:TPU:2, one launch (start us, length us, event | category | flops | bytes accessed | tf_op | source)
XLA Modules:
  0.0 145.3 jit_solution(550045338636112363)
XLA Ops:
  0.6 0.8 pad_maximum_fusion.6
  1.4 4.0 %collective-permute-start = (bf16[128,256]{1,0:T(8,128)(2,1)S(1)}, bf16[128,256]{1,0:T(8,128)(2,1)S(1)}, u32[]{:S(2)}, u32[]{:S(2)}) collective-permute-start(bf16[128,256]{1,0:T(8,128)(2,1)S(1)} %pad_maximum_fusion.6), channel_id=1, source_target_pairs={{0,1},{1,0},{2,3},{3,2},{4,5},{5,4},{6,7},{7,6},{8,9},{9,8},{10,11... | collective-permute-start | bytes 196616 | tf_op jit(solution)/shard_map/ppermute | solution.py:152
  5.5 3.2 %copy.13 = bf16[1,128,8192]{1,2,0:T(8,128)(2,1)S(1)} copy(bf16[1,128,8192]{2,1,0:T(8,128)(2,1)} %param.7) | data formatting | bytes 4194304 | tf_op args[0]
  8.7 0.0 copy-start.3
  8.7 0.0 copy-start.4
  8.7 0.0 copy-start
  8.7 0.0 copy-start.1
  8.7 0.0 copy-start.2
  8.7 1.2 constant_dynamic-slice_fusion.7
  9.9 1.9 %collective-permute-start.6 = (bf16[4096,128]{1,0:T(8,128)(2,1)}, bf16[4096,128]{1,0:T(8,128)(2,1)}, u32[]{:S(2)}, u32[]{:S(2)}) collective-permute-start(bf16[4096,128]{1,0:T(8,128)(2,1)} %bitcast.15), channel_id=1, source_target_pairs={{0,16},{16,0},{1,17},{17,1},{2,18},{18,2},{3,19},{19,3},{4,20},{20... | collective-permute-start | bytes 3145736 | tf_op jit(solution)/shard_map/ppermute | solution.py:152
  11.8 0.0 collective-permute-done
  11.8 0.0 copy-done.3
  11.9 0.0 copy-done.4
  11.9 6.2 %collective-permute-start.4 = (bf16[256,256]{1,0:T(8,128)(2,1)S(1)}, bf16[256,256]{1,0:T(8,128)(2,1)S(1)}, u32[]{:S(2)}, u32[]{:S(2)}) collective-permute-start(bf16[256,256]{1,0:T(8,128)(2,1)S(1)} %pad_maximum_fusion.5.refs_5_), channel_id=1, source_target_pairs={{0,12},{2,14},{4,0},{6,2},{1,13},{3,15},{5,1},{7,3},{16,28},{18,30... | collective-permute-start | bytes 393224 | tf_op jit(solution)/shard_map/ppermute | solution.py:193
  18.1 1.6 %collective-permute-start.3 = (bf16[256,256]{1,0:T(8,128)(2,1)S(1)}, bf16[256,256]{1,0:T(8,128)(2,1)S(1)}, u32[]{:S(2)}, u32[]{:S(2)}) collective-permute-start(bf16[256,256]{1,0:T(8,128)(2,1)S(1)} %pad_maximum_fusion.5.refs_5_), channel_id=1, source_target_pairs={{0,6},{2,8},{4,10},{6,12},{8,14},{1,7},{3,9},{5,11},{7,13},{9,15},... | collective-permute-start | bytes 393224 | tf_op jit(solution)/shard_map/ppermute | solution.py:148
  19.7 3.2 %collective-permute-start.2 = (bf16[256,256]{1,0:T(8,128)(2,1)S(1)}, bf16[256,256]{1,0:T(8,128)(2,1)S(1)}, u32[]{:S(2)}, u32[]{:S(2)}) collective-permute-start(bf16[256,256]{1,0:T(8,128)(2,1)S(1)} %pad_maximum_fusion.5.refs_5_), channel_id=1, source_target_pairs={{0,4},{2,6},{4,8},{6,10},{8,12},{10,14},{1,5},{3,7},{5,9},{7,11},{... | collective-permute-start | bytes 393224 | tf_op jit(solution)/shard_map/ppermute | solution.py:148
  22.9 3.2 %collective-permute-start.1 = (bf16[256,256]{1,0:T(8,128)(2,1)S(1)}, bf16[256,256]{1,0:T(8,128)(2,1)S(1)}, u32[]{:S(2)}, u32[]{:S(2)}) collective-permute-start(bf16[256,256]{1,0:T(8,128)(2,1)S(1)} %pad_maximum_fusion.5.refs_5_), channel_id=1, source_target_pairs={{0,2},{2,4},{4,6},{6,8},{8,10},{10,12},{12,14},{1,3},{3,5},{5,7},{... | collective-permute-start | bytes 393224 | tf_op jit(solution)/shard_map/ppermute | solution.py:148
  26.2 0.0 collective-permute-done.4
  26.2 4.6 %collective-permute-start.5 = (bf16[256,256]{1,0:T(8,128)(2,1)S(1)}, bf16[256,256]{1,0:T(8,128)(2,1)S(1)}, u32[]{:S(2)}, u32[]{:S(2)}) collective-permute-start(bf16[256,256]{1,0:T(8,128)(2,1)S(1)} %collective-permute-done.4), channel_id=1, source_target_pairs={{12,8},{14,10},{0,12},{2,14},{13,9},{15,11},{1,13},{3,15},{28,24},... | collective-permute-start | bytes 393224 | tf_op jit(solution)/shard_map/ppermute | solution.py:194
  31.5 0.1 pad_add_fusion.refs_0_
  31.5 0.0 collective-permute-done.3.refs_8_
  31.5 0.0 collective-permute-done.2.refs_7_
  31.5 0.0 collective-permute-done.1.refs_6_
  31.6 3.6 %collective-permute-done.5.refs_9_ = bf16[256,256]{1,0:T(8,128)(2,1)S(1)} collective-permute-done((bf16[256,256]{1,0:T(8,128)(2,1)S(1)}, bf16[256,256]{1,0:T(8,128)(2,1)S(1)}, u32[]{:S(2)}, u32[]{:S(2)}) %collective-permute-start.5) | collective-permute-done | bytes 131104 | tf_op jit(solution)/shard_map/ppermute | solution.py:194
  35.2 0.0 copy-done
  35.2 0.0 copy-done.1
  35.2 0.0 copy-done.2
  35.2 7.0 %window_attention.1 = (bf16[128,1024]{1,0:T(8,128)(2,1)}, f32[256,256]{1,0:T(8,128)S(1)}, bf16[256,256]{1,0:T(8,128)(2,1)S(1)}, bf16[256,256]{1,0:T(8,128)(2,1)S...) custom-call(s32[2]{0:T(128)S(1)} %pad_add_fusion.refs_0_, s32[1]{0:T(128)S(6)} %copy.14.refs_1_, ...), custom_call_target="tpu_custom_call" | custom-call | flops 1677721600 | bytes 1310720 | tf_op jit(solution)/shard_map/window_attention/pallas_call | solution.py:89
  42.2 1.3 collective-permute-start.10
  43.4 1.3 collective-permute-start.11
  44.7 1.3 collective-permute-start.12
  46.0 1.3 collective-permute-start.13
  47.3 0.2 constant_dynamic-slice_fusion.1
  47.6 1.9 %collective-permute-done.10 = bf16[256,256]{1,0:T(8,128)(2,1)S(1)} collective-permute-done((bf16[256,256]{1,0:T(8,128)(2,1)S(1)}, bf16[256,256]{1,0:T(8,128)(2,1)S(1)}, u32[]{:S(2)}, u32[]{:S(2)}) %collective-permute-start.10) | collective-permute-done | bytes 131104 | tf_op jit(solution)/shard_map/ppermute | solution.py:148
  49.5 7.1 %collective-permute-done.11 = bf16[256,256]{1,0:T(8,128)(2,1)S(1)} collective-permute-done((bf16[256,256]{1,0:T(8,128)(2,1)S(1)}, bf16[256,256]{1,0:T(8,128)(2,1)S(1)}, u32[]{:S(2)}, u32[]{:S(2)}) %collective-permute-start.11) | collective-permute-done | bytes 131104 | tf_op jit(solution)/shard_map/ppermute | solution.py:148
  56.5 6.8 %collective-permute-done.12 = bf16[256,256]{1,0:T(8,128)(2,1)S(1)} collective-permute-done((bf16[256,256]{1,0:T(8,128)(2,1)S(1)}, bf16[256,256]{1,0:T(8,128)(2,1)S(1)}, u32[]{:S(2)}, u32[]{:S(2)}) %collective-permute-start.12) | collective-permute-done | bytes 131104 | tf_op jit(solution)/shard_map/ppermute | solution.py:148
  63.4 0.0 collective-permute-done.13
  63.4 0.1 fusion
  63.5 3.3 %collective-permute-start.14 = (bf16[256,256]{1,0:T(8,128)(2,1)S(1)}, bf16[256,256]{1,0:T(8,128)(2,1)S(1)}, u32[]{:S(2)}, u32[]{:S(2)}) collective-permute-start(bf16[256,256]{1,0:T(8,128)(2,1)S(1)} %fusion), channel_id=1, source_target_pairs={{0,1},{1,0},{2,3},{3,2},{4,5},{5,4},{6,7},{7,6},{8,9},{9,8},{10,11... | collective-permute-start | bytes 393224 | tf_op jit(solution)/shard_map/ppermute | solution.py:152
  66.8 0.0 collective-permute-done.6
  66.8 1.4 constant_dynamic-slice_fusion
  68.2 0.1 pad_maximum_fusion.1
  68.3 4.0 %collective-permute-start.7 = (bf16[1024,256]{1,0:T(8,128)(2,1)S(1)}, bf16[1024,256]{1,0:T(8,128)(2,1)S(1)}, u32[]{:S(2)}, u32[]{:S(2)}) collective-permute-start(bf16[1024,256]{1,0:T(8,128)(2,1)S(1)} %pad_maximum_fusion.1), channel_id=1, source_target_pairs={{0,1},{1,0},{256,257},{257,256},{2,3},{3,2},{258,259},{259,258},{4... | collective-permute-start | bytes 1572872 | tf_op jit(solution)/shard_map/ppermute | solution.py:157
  72.3 0.9 pad_maximum_fusion.2
  73.2 3.3 %collective-permute-start.8 = (bf16[1024,256]{1,0:T(8,128)(2,1)}, bf16[1024,256]{1,0:T(8,128)(2,1)S(1)}, u32[]{:S(2)}, u32[]{:S(2)}) collective-permute-start(bf16[1024,256]{1,0:T(8,128)(2,1)} %pad_maximum_fusion.2), channel_id=1, source_target_pairs={{0,256},{1,257},{256,0},{257,1},{2,258},{3,259},{258,2},{259,3},{4... | collective-permute-start | bytes 1572872 | tf_op jit(solution)/shard_map/ppermute | solution.py:157
  76.5 0.9 pad_maximum_fusion.3
  77.4 2.4 %collective-permute-start.9 = (bf16[1024,256]{1,0:T(8,128)(2,1)}, bf16[1024,256]{1,0:T(8,128)(2,1)S(1)}, u32[]{:S(2)}, u32[]{:S(2)}) collective-permute-start(bf16[1024,256]{1,0:T(8,128)(2,1)} %pad_maximum_fusion.3), channel_id=1, source_target_pairs={{0,257},{1,256},{256,1},{257,0},{2,259},{3,258},{258,3},{259,2},{4... | collective-permute-start | bytes 1572872 | tf_op jit(solution)/shard_map/ppermute | solution.py:157
  79.8 0.0 collective-permute-done.14
  79.8 0.1 add_convert_fusion.refs_4_
  79.9 1.9 %collective-permute-start.15 = (bf16[256,256]{1,0:T(8,128)(2,1)S(1)}, bf16[256,256]{1,0:T(8,128)(2,1)S(1)}, u32[]{:S(2)}, u32[]{:S(2)}) collective-permute-start(bf16[256,256]{1,0:T(8,128)(2,1)S(1)} %add_convert_fusion.refs_4_), channel_id=1, source_target_pairs={{0,16},{16,0},{1,17},{17,1},{2,18},{18,2},{3,19},{19,3},{4,20},{20... | collective-permute-start | bytes 393224 | tf_op jit(solution)/shard_map/ppermute | solution.py:152
  81.8 1.3 collective-permute-done.15.refs_5_
  83.2 2.5 %collective-permute-start.16 = (bf16[2,256,256]{2,1,0:T(8,128)(2,1)S(1)}, bf16[2,256,256]{2,1,0:T(8,128)(2,1)S(1)}, u32[]{:S(2)}, u32[]{:S(2)}) collective-permute-start(bf16[2,256,256]{2,1,0:T(8,128)(2,1)S(1)} %pad_maximum_fusion.4), channel_id=1, source_target_pairs={{0,256},{256,0},{1,257},{257,1},{2,258},{258,2},{3,259},{259,3},{4... | collective-permute-start | bytes 786440 | tf_op jit(solution)/shard_map/ppermute | solution.py:152
  85.7 0.1 pad_add_fusion.1.at_ref
  85.8 0.1 pad_maximum_fusion.refs_0_
  85.9 13.3 %collective-permute-done.16.refs_6_ = bf16[2,256,256]{2,1,0:T(8,128)(2,1)S(1)} collective-permute-done((bf16[2,256,256]{2,1,0:T(8,128)(2,1)S(1)}, bf16[2,256,256]{2,1,0:T(8,128)(2,1)S(1)}, u32[]{:S(2)}, u32[]{:S(2)}) %collective-permute-start.16) | collective-permute-done | bytes 262176 | tf_op jit(solution)/shard_map/ppermute | solution.py:152
  99.2 0.0 collective-permute-done.7.refs_1_
  99.2 0.0 collective-permute-done.8.refs_2_
  99.2 0.0 collective-permute-done.9.refs_3_
  99.2 1.8 %weight_partials.1 = bf16[1024,256]{1,0:T(8,128)(2,1)S(1)} custom-call(s32[2]{0:T(128)S(1)} %pad_add_fusion.1.at_ref, bf16[1024,256]{1,0:T(8,128)(2,1)S(1)} %pad_maximum_fusion.refs_0_, bf16[1024,256]{1,0:T(8,128)(2,1)S(1)} %collective-permute-done.7.refs_1_, bf16[1024,256]{1,0:T(8,128)(2,1)S(1)} %collective-permute-done.8.refs_2_, ...), custom_call_target="tpu_custom_call" | custom-call | flops 536870912 | bytes 2621440 | tf_op jit(solution)/shard_map/weight_partials/pallas_call | solution.py:127
  101.1 43.5 %all_to_all.5 = bf16[64,16,256]{2,1,0:T(8,128)(2,1)S(1)} all-to-all(bf16[64,16,256]{2,1,0:T(8,128)(2,1)S(1)} %bitcast.27), channel_id=1, replica_groups=mesh['x_lo'=2,'z'=8,'core'=2,'y'=8,'x_hi'=2] {'z','y'}, dimensions={0} | all-to-all | bytes 1048576 | tf_op jit(solution)/shard_map/all_to_all | solution.py:243
  144.5 0.1 convert_reduce_fusion
  144.6 0.6 multiply_convert_fusion
  (3 shorter events, 0.1 us)
Async XLA Ops:
  1.4 10.4 %collective-permute-start = (bf16[128,256]{1,0:T(8,128)(2,1)S(1)}, bf16[128,256]{1,0:T(8,128)(2,1)S(1)}, u32[]{:S(2)}, u32[]{:S(2)}) collective-permute-start(bf16[128,256]{1,0:T(8,128)(2,1)S(1)} %pad_maximum_fusion.6), channel_id=1, source_target_pairs={{0,1},{1,0},{2,3},{3,2},{4,5},{5,4},{6,7},{7,6},{8,9},{9,8},{10,11... | collective-permute-start | bytes 196616 | tf_op jit(solution)/shard_map/ppermute | solution.py:152
  8.7 3.2 %copy-start.3 = (bf16[1,128,128]{2,1,0:T(8,128)(2,1)S(1)}, bf16[1,128,128]{2,1,0:T(8,128)(2,1)}, u32[]{:S(2)}) copy-start(bf16[1,128,128]{2,1,0:T(8,128)(2,1)} %param.10) | copy-start | bytes 98308
  8.7 3.2 %copy-start.4 = (bf16[1,128,128]{2,1,0:T(8,128)(2,1)S(1)}, bf16[1,128,128]{2,1,0:T(8,128)(2,1)}, u32[]{:S(2)}) copy-start(bf16[1,128,128]{2,1,0:T(8,128)(2,1)} %param.9) | copy-start | bytes 98308
  8.7 26.5 %copy-start = (bf16[1,128,1024]{2,1,0:T(8,128)(2,1)S(1)}, bf16[1,128,1024]{2,1,0:T(8,128)(2,1)}, u32[]{:S(2)}) copy-start(bf16[1,128,1024]{2,1,0:T(8,128)(2,1)} %param.8) | copy-start | bytes 786436
  8.7 26.5 %copy-start.1 = (bf16[1,128,1024]{2,1,0:T(8,128)(2,1)S(1)}, bf16[1,128,1024]{2,1,0:T(8,128)(2,1)}, u32[]{:S(2)}) copy-start(bf16[1,128,1024]{2,1,0:T(8,128)(2,1)} %param.11) | copy-start | bytes 786436
  8.7 26.5 %copy-start.2 = (s32[1,2048]{1,0:T(1,128)S(1)}, s32[1,2048]{1,0:T(1,128)}, u32[]{:S(2)}) copy-start(s32[1,2048]{1,0:T(1,128)} %refs_2_.1) | copy-start | bytes 24580
  9.9 56.9 %collective-permute-start.6 = (bf16[4096,128]{1,0:T(8,128)(2,1)}, bf16[4096,128]{1,0:T(8,128)(2,1)}, u32[]{:S(2)}, u32[]{:S(2)}) collective-permute-start(bf16[4096,128]{1,0:T(8,128)(2,1)} %bitcast.15), channel_id=1, source_target_pairs={{0,16},{16,0},{1,17},{17,1},{2,18},{18,2},{3,19},{19,3},{4,20},{20... | collective-permute-start | bytes 3145736 | tf_op jit(solution)/shard_map/ppermute | solution.py:152
  11.9 14.2 %collective-permute-start.4 = (bf16[256,256]{1,0:T(8,128)(2,1)S(1)}, bf16[256,256]{1,0:T(8,128)(2,1)S(1)}, u32[]{:S(2)}, u32[]{:S(2)}) collective-permute-start(bf16[256,256]{1,0:T(8,128)(2,1)S(1)} %pad_maximum_fusion.5.refs_5_), channel_id=1, source_target_pairs={{0,12},{2,14},{4,0},{6,2},{1,13},{3,15},{5,1},{7,3},{16,28},{18,30... | collective-permute-start | bytes 393224 | tf_op jit(solution)/shard_map/ppermute | solution.py:193
  18.1 13.5 %collective-permute-start.3 = (bf16[256,256]{1,0:T(8,128)(2,1)S(1)}, bf16[256,256]{1,0:T(8,128)(2,1)S(1)}, u32[]{:S(2)}, u32[]{:S(2)}) collective-permute-start(bf16[256,256]{1,0:T(8,128)(2,1)S(1)} %pad_maximum_fusion.5.refs_5_), channel_id=1, source_target_pairs={{0,6},{2,8},{4,10},{6,12},{8,14},{1,7},{3,9},{5,11},{7,13},{9,15},... | collective-permute-start | bytes 393224 | tf_op jit(solution)/shard_map/ppermute | solution.py:148
  19.7 11.8 %collective-permute-start.2 = (bf16[256,256]{1,0:T(8,128)(2,1)S(1)}, bf16[256,256]{1,0:T(8,128)(2,1)S(1)}, u32[]{:S(2)}, u32[]{:S(2)}) collective-permute-start(bf16[256,256]{1,0:T(8,128)(2,1)S(1)} %pad_maximum_fusion.5.refs_5_), channel_id=1, source_target_pairs={{0,4},{2,6},{4,8},{6,10},{8,12},{10,14},{1,5},{3,7},{5,9},{7,11},{... | collective-permute-start | bytes 393224 | tf_op jit(solution)/shard_map/ppermute | solution.py:148
  22.9 8.6 %collective-permute-start.1 = (bf16[256,256]{1,0:T(8,128)(2,1)S(1)}, bf16[256,256]{1,0:T(8,128)(2,1)S(1)}, u32[]{:S(2)}, u32[]{:S(2)}) collective-permute-start(bf16[256,256]{1,0:T(8,128)(2,1)S(1)} %pad_maximum_fusion.5.refs_5_), channel_id=1, source_target_pairs={{0,2},{2,4},{4,6},{6,8},{8,10},{10,12},{12,14},{1,3},{3,5},{5,7},{... | collective-permute-start | bytes 393224 | tf_op jit(solution)/shard_map/ppermute | solution.py:148
  26.2 9.0 %collective-permute-start.5 = (bf16[256,256]{1,0:T(8,128)(2,1)S(1)}, bf16[256,256]{1,0:T(8,128)(2,1)S(1)}, u32[]{:S(2)}, u32[]{:S(2)}) collective-permute-start(bf16[256,256]{1,0:T(8,128)(2,1)S(1)} %collective-permute-done.4), channel_id=1, source_target_pairs={{12,8},{14,10},{0,12},{2,14},{13,9},{15,11},{1,13},{3,15},{28,24},... | collective-permute-start | bytes 393224 | tf_op jit(solution)/shard_map/ppermute | solution.py:194
  42.2 7.3 %collective-permute-start.10 = (bf16[256,256]{1,0:T(8,128)(2,1)S(1)}, bf16[256,256]{1,0:T(8,128)(2,1)S(1)}, u32[]{:S(2)}, u32[]{:S(2)}) collective-permute-start(bf16[256,256]{1,0:T(8,128)(2,1)S(1)} %get-tuple-element.10), channel_id=1, source_target_pairs={{2,0},{4,2},{6,4},{8,6},{10,8},{12,10},{14,12},{3,1},{5,3},{7,5},{... | collective-permute-start | bytes 393224 | tf_op jit(solution)/shard_map/ppermute | solution.py:148
  43.4 13.1 %collective-permute-start.11 = (bf16[256,256]{1,0:T(8,128)(2,1)S(1)}, bf16[256,256]{1,0:T(8,128)(2,1)S(1)}, u32[]{:S(2)}, u32[]{:S(2)}) collective-permute-start(bf16[256,256]{1,0:T(8,128)(2,1)S(1)} %get-tuple-element.11), channel_id=1, source_target_pairs={{4,0},{6,2},{8,4},{10,6},{12,8},{14,10},{5,1},{7,3},{9,5},{11,7},{... | collective-permute-start | bytes 393224 | tf_op jit(solution)/shard_map/ppermute | solution.py:148
  44.7 18.7 %collective-permute-start.12 = (bf16[256,256]{1,0:T(8,128)(2,1)S(1)}, bf16[256,256]{1,0:T(8,128)(2,1)S(1)}, u32[]{:S(2)}, u32[]{:S(2)}) collective-permute-start(bf16[256,256]{1,0:T(8,128)(2,1)S(1)} %get-tuple-element.12), channel_id=1, source_target_pairs={{6,0},{8,2},{10,4},{12,6},{14,8},{7,1},{9,3},{11,5},{13,7},{15,9},... | collective-permute-start | bytes 393224 | tf_op jit(solution)/shard_map/ppermute | solution.py:148
  46.0 17.4 %collective-permute-start.13 = (bf16[256,256]{1,0:T(8,128)(2,1)S(1)}, bf16[256,256]{1,0:T(8,128)(2,1)S(1)}, u32[]{:S(2)}, u32[]{:S(2)}) collective-permute-start(bf16[256,256]{1,0:T(8,128)(2,1)S(1)} %get-tuple-element.13), channel_id=1, source_target_pairs={{8,0},{10,2},{12,4},{14,6},{9,1},{11,3},{13,5},{15,7},{24,16},{26,... | collective-permute-start | bytes 393224 | tf_op jit(solution)/shard_map/ppermute | solution.py:148
  63.5 16.3 %collective-permute-start.14 = (bf16[256,256]{1,0:T(8,128)(2,1)S(1)}, bf16[256,256]{1,0:T(8,128)(2,1)S(1)}, u32[]{:S(2)}, u32[]{:S(2)}) collective-permute-start(bf16[256,256]{1,0:T(8,128)(2,1)S(1)} %fusion), channel_id=1, source_target_pairs={{0,1},{1,0},{2,3},{3,2},{4,5},{5,4},{6,7},{7,6},{8,9},{9,8},{10,11... | collective-permute-start | bytes 393224 | tf_op jit(solution)/shard_map/ppermute | solution.py:152
  68.3 30.9 %collective-permute-start.7 = (bf16[1024,256]{1,0:T(8,128)(2,1)S(1)}, bf16[1024,256]{1,0:T(8,128)(2,1)S(1)}, u32[]{:S(2)}, u32[]{:S(2)}) collective-permute-start(bf16[1024,256]{1,0:T(8,128)(2,1)S(1)} %pad_maximum_fusion.1), channel_id=1, source_target_pairs={{0,1},{1,0},{256,257},{257,256},{2,3},{3,2},{258,259},{259,258},{4... | collective-permute-start | bytes 1572872 | tf_op jit(solution)/shard_map/ppermute | solution.py:157
  73.2 26.0 %collective-permute-start.8 = (bf16[1024,256]{1,0:T(8,128)(2,1)}, bf16[1024,256]{1,0:T(8,128)(2,1)S(1)}, u32[]{:S(2)}, u32[]{:S(2)}) collective-permute-start(bf16[1024,256]{1,0:T(8,128)(2,1)} %pad_maximum_fusion.2), channel_id=1, source_target_pairs={{0,256},{1,257},{256,0},{257,1},{2,258},{3,259},{258,2},{259,3},{4... | collective-permute-start | bytes 1572872 | tf_op jit(solution)/shard_map/ppermute | solution.py:157
  77.4 21.9 %collective-permute-start.9 = (bf16[1024,256]{1,0:T(8,128)(2,1)}, bf16[1024,256]{1,0:T(8,128)(2,1)S(1)}, u32[]{:S(2)}, u32[]{:S(2)}) collective-permute-start(bf16[1024,256]{1,0:T(8,128)(2,1)} %pad_maximum_fusion.3), channel_id=1, source_target_pairs={{0,257},{1,256},{256,1},{257,0},{2,259},{3,258},{258,3},{259,2},{4... | collective-permute-start | bytes 1572872 | tf_op jit(solution)/shard_map/ppermute | solution.py:157
  79.9 3.2 %collective-permute-start.15 = (bf16[256,256]{1,0:T(8,128)(2,1)S(1)}, bf16[256,256]{1,0:T(8,128)(2,1)S(1)}, u32[]{:S(2)}, u32[]{:S(2)}) collective-permute-start(bf16[256,256]{1,0:T(8,128)(2,1)S(1)} %add_convert_fusion.refs_4_), channel_id=1, source_target_pairs={{0,16},{16,0},{1,17},{17,1},{2,18},{18,2},{3,19},{19,3},{4,20},{20... | collective-permute-start | bytes 393224 | tf_op jit(solution)/shard_map/ppermute | solution.py:152
  83.2 16.0 %collective-permute-start.16 = (bf16[2,256,256]{2,1,0:T(8,128)(2,1)S(1)}, bf16[2,256,256]{2,1,0:T(8,128)(2,1)S(1)}, u32[]{:S(2)}, u32[]{:S(2)}) collective-permute-start(bf16[2,256,256]{2,1,0:T(8,128)(2,1)S(1)} %pad_maximum_fusion.4), channel_id=1, source_target_pairs={{0,256},{256,0},{1,257},{257,1},{2,258},{258,2},{3,259},{259,3},{4... | collective-permute-start | bytes 786440 | tf_op jit(solution)/shard_map/ppermute | solution.py:152
where the time goes:
time: 146 us; the launch traced here: 145 us
  starting transfers between devices  47.5 us (33%)
  blocking collectives  43.5 us (30%)
  waiting for transfers between devices  34.2 us (23%)
  Pallas kernels  8.81 us (6%)
  local copies, waits for them, and re-layouts  6.01 us (4%)
  other arithmetic  3.71 us (3%)
  between operations  1.63 us (1%)
    all_to_all x1, blocking collectives, step(): lax.all_to_all(pieces, ('z', 'y'), split_axis=0, concat_axis=0, tiled=True)  43.5 us
    ppermute x7, waiting for transfers between devices, y_shift(): lax.ppermute(x, 'y', [(i, i + by) for i in range(count) if 0 <= i + by <...  15.9 us
    ppermute x5, waiting for transfers between devices, flipped(): return lax.ppermute(x, axis, [(0, 1), (1, 0)])  14.7 us
    ppermute x5, starting transfers between devices, flipped(): return lax.ppermute(x, axis, [(0, 1), (1, 0)])  13.7 us
    ppermute x7, starting transfers between devices, y_shift(): lax.ppermute(x, 'y', [(i, i + by) for i in range(count) if 0 <= i + by <...  13.2 us
    ppermute x3, starting transfers between devices, x_swap(): return lax.ppermute(x, ('x_lo', 'x_hi'), pairs)  9.79 us
    pallas_call x1, Pallas kernels, attention(): pl.pallas_call(kernel, out_shape=[jax.ShapeDtypeStruct((rows, wide), BF16...  6.96 us
    ppermute x1, starting transfers between devices, step(): passing = lax.ppermute(both, 'y', first)  6.16 us
  transfers between devices with their start and end apart: 17, of which 6 were waited for; matrix products, arithmetic and copies ran while one was open for 6% of the time, Pallas kernels for 5%

commit v1 on v0

--- a/solution.py
+++ b/solution.py
@@ -106,15 +106,12 @@
 
 
 def weights_kernel(at_ref, *refs):
-    inputs, grads, out_ref = refs[:4], refs[4:7], refs[7]
+    inputs, grads, out_ref = refs[:4], refs[4:8], refs[8]
     rows = grads[0].shape[0] // 2
     total = None
     for n, x in enumerate(inputs):
         at = pl.ds(pl.multiple_of(at_ref[n % 2] * rows, rows), rows)
-        if n < 2:
-            parts = [grads[0][at, :], grads[1][at, :]]
-        else:
-            parts = [grads[2][0, at, :], grads[2][1, at, :]]
+        parts = [g[at, :] for g in grads[n // 2 * 2 :][:2]]
         term = contract(x[...], jnp.concatenate(parts, axis=0), 1, 0)
         total = term if total is None else total + term
     out_ref[...] = total.astype(BF16)
@@ -130,8 +127,7 @@
         grid=(steps,),
         in_specs=[pl.BlockSpec(memory_space=pltpu.SMEM)]
         + [pl.BlockSpec((tall, deep), lambda j: (j, 0))] * 4
-        + [pl.BlockSpec(grads[0].shape, lambda j: (0, 0))] * 2
-        + [pl.BlockSpec(grads[2].shape, lambda j: (0, 0, 0))],
+        + [pl.BlockSpec(grads[0].shape, lambda j: (0, 0))] * 4,
         out_specs=pl.BlockSpec((tall, wide), lambda j: (j, 0)),
         cost_estimate=pl.CostEstimate(
             flops=2 * count * wide * deep * 4,
@@ -233,10 +229,11 @@
         total = total + came.astype(F32)
     came = flipped(total.astype(BF16), "x_hi")
     grad_kv = (total + came.astype(F32)).astype(BF16)
-    core_grad = flipped(grad_kv, "core")
-    x_grads = flipped(jnp.stack([grad_kv, core_grad]), "x_lo")
+    grads = [grad_kv]
+    for axes, flip in (("core", 1), ("x_lo", 1), (("x_lo", "core"), 3)):
+        grads.append(lax.ppermute(grad_kv, axes, [(i, i ^ flip) for i in range(flip + 1)]))
     at = jnp.stack([x_hi, 1 - x_hi]).astype(jnp.int32)
-    partial_value = weight_partials(at, inputs, [grad_kv, core_grad, x_grads], 4)
+    partial_value = weight_partials(at, inputs, grads, 4)
 
     peers = z_count * y_count
     pieces = partial_value.reshape(peers, fine, 2 * head_size)

time: 146 us -> 149 us (1.021)
  the two profiles are of different devices: /device:TPU:2 before, /device:TPU:8 now
where the time goes in v1:
time: 149 us; the launch traced here: 148 us
  starting transfers between devices  52.7 us (35%)
  waiting for transfers between devices  44.4 us (30%)
  blocking collectives  31.9 us (21%)
  Pallas kernels  8.81 us (6%)
  local copies, waits for them, and re-layouts  6.01 us (4%)
  other arithmetic  2.9 us (2%)
  between operations  1.64 us (1%)
    all_to_all x1, blocking collectives, step(): lax.all_to_all(pieces, ('z', 'y'), split_axis=0, concat_axis=0, tiled=True)  31.9 us
    ppermute x7, waiting for transfers between devices, y_shift(): lax.ppermute(x, 'y', [(i, i + by) for i in range(count) if 0 <= i + by <...  29.1 us
    ppermute x7, starting transfers between devices, y_shift(): lax.ppermute(x, 'y', [(i, i + by) for i in range(count) if 0 <= i + by <...  15.7 us
    ppermute x3, waiting for transfers between devices, step(): lax.ppermute(grad_kv, axes, [(i, i ^ flip) for i in range(flip + 1)])  15.3 us
    ppermute x3, starting transfers between devices, x_swap(): return lax.ppermute(x, ('x_lo', 'x_hi'), pairs)  9.81 us
    ppermute x3, starting transfers between devices, flipped(): return lax.ppermute(x, axis, [(0, 1), (1, 0)])  9.58 us
    ppermute x3, starting transfers between devices, step(): lax.ppermute(grad_kv, axes, [(i, i ^ flip) for i in range(flip + 1)])  7.74 us
    pallas_call x1, Pallas kernels, attention(): pl.pallas_call(kernel, out_shape=[jax.ShapeDtypeStruct((rows, wide), BF16...  6.96 us
  transfers between devices with their start and end apart: 18, of which 8 were waited for; matrix products, arithmetic and copies ran while one was open for 5% of the time, Pallas kernels for 5%

profile of v1, /device:TPU:8, one launch (start us, length us, event | category | flops | bytes accessed | tf_op | source)
XLA Modules:
  0.0 148.4 jit_solution(1762312528723267497)
XLA Ops:
  0.6 0.8 pad_maximum_fusion.5
  1.4 4.9 %collective-permute-start = (bf16[128,256]{1,0:T(8,128)(2,1)S(1)}, bf16[128,256]{1,0:T(8,128)(2,1)S(1)}, u32[]{:S(2)}, u32[]{:S(2)}) collective-permute-start(bf16[128,256]{1,0:T(8,128)(2,1)S(1)} %pad_maximum_fusion.5), channel_id=1, source_target_pairs={{0,1},{1,0},{2,3},{3,2},{4,5},{5,4},{6,7},{7,6},{8,9},{9,8},{10,11... | collective-permute-start | bytes 196616 | tf_op jit(solution)/shard_map/ppermute | solution.py:148
  6.4 3.2 %copy.13 = bf16[1,128,8192]{1,2,0:T(8,128)(2,1)S(1)} copy(bf16[1,128,8192]{2,1,0:T(8,128)(2,1)} %param.7) | data formatting | bytes 4194304 | tf_op args[0]
  9.6 0.0 copy-start.3
  9.6 0.0 copy-start.4
  9.6 0.0 copy-start
  9.6 0.0 copy-start.1
  9.6 0.0 copy-start.2
  9.6 1.2 constant_dynamic-slice_fusion.7
  10.8 1.9 %collective-permute-start.6 = (bf16[4096,128]{1,0:T(8,128)(2,1)}, bf16[4096,128]{1,0:T(8,128)(2,1)}, u32[]{:S(2)}, u32[]{:S(2)}) collective-permute-start(bf16[4096,128]{1,0:T(8,128)(2,1)} %bitcast.15), channel_id=1, source_target_pairs={{0,16},{16,0},{1,17},{17,1},{2,18},{18,2},{3,19},{19,3},{4,20},{20... | collective-permute-start | bytes 3145736 | tf_op jit(solution)/shard_map/ppermute | solution.py:148
  12.7 0.0 collective-permute-done
  12.7 0.0 copy-done.3
  12.8 0.0 copy-done.4
  12.8 5.3 %collective-permute-start.4 = (bf16[256,256]{1,0:T(8,128)(2,1)S(1)}, bf16[256,256]{1,0:T(8,128)(2,1)S(1)}, u32[]{:S(2)}, u32[]{:S(2)}) collective-permute-start(bf16[256,256]{1,0:T(8,128)(2,1)S(1)} %pad_maximum_fusion.4.refs_5_), channel_id=1, source_target_pairs={{0,12},{2,14},{4,0},{6,2},{1,13},{3,15},{5,1},{7,3},{16,28},{18,30... | collective-permute-start | bytes 393224 | tf_op jit(solution)/shard_map/ppermute | solution.py:189
  18.1 2.1 %collective-permute-start.3 = (bf16[256,256]{1,0:T(8,128)(2,1)S(1)}, bf16[256,256]{1,0:T(8,128)(2,1)S(1)}, u32[]{:S(2)}, u32[]{:S(2)}) collective-permute-start(bf16[256,256]{1,0:T(8,128)(2,1)S(1)} %pad_maximum_fusion.4.refs_5_), channel_id=1, source_target_pairs={{0,6},{2,8},{4,10},{6,12},{8,14},{1,7},{3,9},{5,11},{7,13},{9,15},... | collective-permute-start | bytes 393224 | tf_op jit(solution)/shard_map/ppermute | solution.py:144
  20.2 3.3 %collective-permute-start.2 = (bf16[256,256]{1,0:T(8,128)(2,1)S(1)}, bf16[256,256]{1,0:T(8,128)(2,1)S(1)}, u32[]{:S(2)}, u32[]{:S(2)}) collective-permute-start(bf16[256,256]{1,0:T(8,128)(2,1)S(1)} %pad_maximum_fusion.4.refs_5_), channel_id=1, source_target_pairs={{0,4},{2,6},{4,8},{6,10},{8,12},{10,14},{1,5},{3,7},{5,9},{7,11},{... | collective-permute-start | bytes 393224 | tf_op jit(solution)/shard_map/ppermute | solution.py:144
  23.6 2.6 %collective-permute-start.1 = (bf16[256,256]{1,0:T(8,128)(2,1)S(1)}, bf16[256,256]{1,0:T(8,128)(2,1)S(1)}, u32[]{:S(2)}, u32[]{:S(2)}) collective-permute-start(bf16[256,256]{1,0:T(8,128)(2,1)S(1)} %pad_maximum_fusion.4.refs_5_), channel_id=1, source_target_pairs={{0,2},{2,4},{4,6},{6,8},{8,10},{10,12},{12,14},{1,3},{3,5},{5,7},{... | collective-permute-start | bytes 393224 | tf_op jit(solution)/shard_map/ppermute | solution.py:144
  26.1 0.0 collective-permute-done.4
  26.2 4.6 %collective-permute-start.5 = (bf16[256,256]{1,0:T(8,128)(2,1)S(1)}, bf16[256,256]{1,0:T(8,128)(2,1)S(1)}, u32[]{:S(2)}, u32[]{:S(2)}) collective-permute-start(bf16[256,256]{1,0:T(8,128)(2,1)S(1)} %collective-permute-done.4), channel_id=1, source_target_pairs={{12,8},{14,10},{0,12},{2,14},{13,9},{15,11},{1,13},{3,15},{28,24},... | collective-permute-start | bytes 393224 | tf_op jit(solution)/shard_map/ppermute | solution.py:190
  31.5 0.1 pad_add_fusion.refs_0_
  31.5 0.0 collective-permute-done.3.refs_8_
  31.5 0.6 collective-permute-done.2.refs_7_
  32.2 2.8 %collective-permute-done.1.refs_6_ = bf16[256,256]{1,0:T(8,128)(2,1)S(1)} collective-permute-done((bf16[256,256]{1,0:T(8,128)(2,1)S(1)}, bf16[256,256]{1,0:T(8,128)(2,1)S(1)}, u32[]{:S(2)}, u32[]{:S(2)}) %collective-permute-start.1) | collective-permute-done | bytes 131104 | tf_op jit(solution)/shard_map/ppermute | solution.py:144
  34.9 0.0 collective-permute-done.5.refs_9_
  34.9 0.0 copy-done
  35.0 0.0 copy-done.1
  35.0 0.0 copy-done.2
  35.0 7.0 %window_attention.1 = (bf16[128,1024]{1,0:T(8,128)(2,1)}, f32[256,256]{1,0:T(8,128)S(1)}, bf16[256,256]{1,0:T(8,128)(2,1)S(1)}, bf16[256,256]{1,0:T(8,128)(2,1)S...) custom-call(s32[2]{0:T(128)S(1)} %pad_add_fusion.refs_0_, s32[1]{0:T(128)S(6)} %copy.14.refs_1_, ...), custom_call_target="tpu_custom_call" | custom-call | flops 1677721600 | bytes 1310720 | tf_op jit(solution)/shard_map/window_attention/pallas_call | solution.py:89
  41.9 3.8 %collective-permute-start.10 = (bf16[256,256]{1,0:T(8,128)(2,1)S(1)}, bf16[256,256]{1,0:T(8,128)(2,1)S(1)}, u32[]{:S(2)}, u32[]{:S(2)}) collective-permute-start(bf16[256,256]{1,0:T(8,128)(2,1)S(1)} %get-tuple-element.10), channel_id=1, source_target_pairs={{2,0},{4,2},{6,4},{8,6},{10,8},{12,10},{14,12},{3,1},{5,3},{7,5},{... | collective-permute-start | bytes 393224 | tf_op jit(solution)/shard_map/ppermute | solution.py:144
  45.7 1.3 collective-permute-start.11
  47.0 1.3 collective-permute-start.12
  48.3 1.3 collective-permute-start.13
  49.6 0.2 constant_dynamic-slice_fusion.1
  49.8 1.6 %collective-permute-done.10 = bf16[256,256]{1,0:T(8,128)(2,1)S(1)} collective-permute-done((bf16[256,256]{1,0:T(8,128)(2,1)S(1)}, bf16[256,256]{1,0:T(8,128)(2,1)S(1)}, u32[]{:S(2)}, u32[]{:S(2)}) %collective-permute-start.10) | collective-permute-done | bytes 131104 | tf_op jit(solution)/shard_map/ppermute | solution.py:144
  51.5 6.7 %collective-permute-done.11 = bf16[256,256]{1,0:T(8,128)(2,1)S(1)} collective-permute-done((bf16[256,256]{1,0:T(8,128)(2,1)S(1)}, bf16[256,256]{1,0:T(8,128)(2,1)S(1)}, u32[]{:S(2)}, u32[]{:S(2)}) %collective-permute-start.11) | collective-permute-done | bytes 131104 | tf_op jit(solution)/shard_map/ppermute | solution.py:144
  58.2 8.3 %collective-permute-done.12 = bf16[256,256]{1,0:T(8,128)(2,1)S(1)} collective-permute-done((bf16[256,256]{1,0:T(8,128)(2,1)S(1)}, bf16[256,256]{1,0:T(8,128)(2,1)S(1)}, u32[]{:S(2)}, u32[]{:S(2)}) %collective-permute-start.12) | collective-permute-done | bytes 131104 | tf_op jit(solution)/shard_map/ppermute | solution.py:144
  66.5 9.0 %collective-permute-done.13 = bf16[256,256]{1,0:T(8,128)(2,1)S(1)} collective-permute-done((bf16[256,256]{1,0:T(8,128)(2,1)S(1)}, bf16[256,256]{1,0:T(8,128)(2,1)S(1)}, u32[]{:S(2)}, u32[]{:S(2)}) %collective-permute-start.13) | collective-permute-done | bytes 131104 | tf_op jit(solution)/shard_map/ppermute | solution.py:144
  75.5 0.1 fusion
  75.6 2.7 %collective-permute-start.14 = (bf16[256,256]{1,0:T(8,128)(2,1)S(1)}, bf16[256,256]{1,0:T(8,128)(2,1)S(1)}, u32[]{:S(2)}, u32[]{:S(2)}) collective-permute-start(bf16[256,256]{1,0:T(8,128)(2,1)S(1)} %fusion), channel_id=1, source_target_pairs={{0,1},{1,0},{2,3},{3,2},{4,5},{5,4},{6,7},{7,6},{8,9},{9,8},{10,11... | collective-permute-start | bytes 393224 | tf_op jit(solution)/shard_map/ppermute | solution.py:148
  78.3 0.0 collective-permute-done.6
  78.4 1.4 constant_dynamic-slice_fusion
  79.8 0.1 pad_maximum_fusion.1
  79.8 4.6 %collective-permute-start.7 = (bf16[1024,256]{1,0:T(8,128)(2,1)S(1)}, bf16[1024,256]{1,0:T(8,128)(2,1)S(1)}, u32[]{:S(2)}, u32[]{:S(2)}) collective-permute-start(bf16[1024,256]{1,0:T(8,128)(2,1)S(1)} %pad_maximum_fusion.1), channel_id=1, source_target_pairs={{0,1},{1,0},{256,257},{257,256},{2,3},{3,2},{258,259},{259,258},{4... | collective-permute-start | bytes 1572872 | tf_op jit(solution)/shard_map/ppermute | solution.py:153
  84.4 0.1 pad_maximum_fusion.2
  84.5 2.5 %collective-permute-start.8 = (bf16[1024,256]{1,0:T(8,128)(2,1)S(1)}, bf16[1024,256]{1,0:T(8,128)(2,1)S(1)}, u32[]{:S(2)}, u32[]{:S(2)}) collective-permute-start(bf16[1024,256]{1,0:T(8,128)(2,1)S(1)} %pad_maximum_fusion.2), channel_id=1, source_target_pairs={{0,256},{1,257},{256,0},{257,1},{2,258},{3,259},{258,2},{259,3},{4... | collective-permute-start | bytes 1572872 | tf_op jit(solution)/shard_map/ppermute | solution.py:153
  87.0 0.9 pad_maximum_fusion.3
  87.9 2.7 %collective-permute-start.9 = (bf16[1024,256]{1,0:T(8,128)(2,1)}, bf16[1024,256]{1,0:T(8,128)(2,1)S(1)}, u32[]{:S(2)}, u32[]{:S(2)}) collective-permute-start(bf16[1024,256]{1,0:T(8,128)(2,1)} %pad_maximum_fusion.3), channel_id=1, source_target_pairs={{0,257},{1,256},{256,1},{257,0},{2,259},{3,258},{258,3},{259,2},{4... | collective-permute-start | bytes 1572872 | tf_op jit(solution)/shard_map/ppermute | solution.py:153
  90.6 0.0 collective-permute-done.14
  90.6 0.1 add_convert_fusion.refs_4_
  90.7 1.9 %collective-permute-start.17 = (bf16[256,256]{1,0:T(8,128)(2,1)S(1)}, bf16[256,256]{1,0:T(8,128)(2,1)S(1)}, u32[]{:S(2)}, u32[]{:S(2)}) collective-permute-start(bf16[256,256]{1,0:T(8,128)(2,1)S(1)} %add_convert_fusion.refs_4_), channel_id=1, source_target_pairs={{0,272},{16,256},{256,16},{272,0},{1,273},{17,257},{257,17},{273,1... | collective-permute-start | bytes 393224 | tf_op jit(solution)/shard_map/ppermute | solution.py:234
  92.6 3.1 %collective-permute-start.16 = (bf16[256,256]{1,0:T(8,128)(2,1)S(1)}, bf16[256,256]{1,0:T(8,128)(2,1)S(1)}, u32[]{:S(2)}, u32[]{:S(2)}) collective-permute-start(bf16[256,256]{1,0:T(8,128)(2,1)S(1)} %add_convert_fusion.refs_4_), channel_id=1, source_target_pairs={{0,256},{256,0},{1,257},{257,1},{2,258},{258,2},{3,259},{259,3},{4... | collective-permute-start | bytes 393224 | tf_op jit(solution)/shard_map/ppermute | solution.py:234
  95.7 14.5 %collective-permute-done.17.refs_7_ = bf16[256,256]{1,0:T(8,128)(2,1)S(1)} collective-permute-done((bf16[256,256]{1,0:T(8,128)(2,1)S(1)}, bf16[256,256]{1,0:T(8,128)(2,1)S(1)}, u32[]{:S(2)}, u32[]{:S(2)}) %collective-permute-start.17) | collective-permute-done | bytes 131104 | tf_op jit(solution)/shard_map/ppermute | solution.py:234
  110.2 2.8 %collective-permute-start.15 = (bf16[256,256]{1,0:T(8,128)(2,1)S(1)}, bf16[256,256]{1,0:T(8,128)(2,1)S(1)}, u32[]{:S(2)}, u32[]{:S(2)}) collective-permute-start(bf16[256,256]{1,0:T(8,128)(2,1)S(1)} %add_convert_fusion.refs_4_), channel_id=1, source_target_pairs={{0,16},{16,0},{1,17},{17,1},{2,18},{18,2},{3,19},{19,3},{4,20},{20... | collective-permute-start | bytes 393224 | tf_op jit(solution)/shard_map/ppermute | solution.py:234
  113.0 0.1 pad_add_fusion.1.at_ref
  113.0 0.1 pad_maximum_fusion.refs_0_
  113.1 0.0 collective-permute-done.16.refs_6_
  113.1 0.8 collective-permute-done.15.refs_5_
  113.9 0.0 collective-permute-done.7.refs_1_
  113.9 0.0 collective-permute-done.8.refs_2_
  113.9 0.0 collective-permute-done.9.refs_3_
  113.9 1.8 %weight_partials.1 = bf16[1024,256]{1,0:T(8,128)(2,1)S(1)} custom-call(s32[2]{0:T(128)S(1)} %pad_add_fusion.1.at_ref, bf16[1024,256]{1,0:T(8,128)(2,1)S(1)} %pad_maximum_fusion.refs_0_, bf16[1024,256]{1,0:T(8,128)(2,1)S(1)} %collective-permute-done.7.refs_1_, bf16[1024,256]{1,0:T(8,128)(2,1)S(1)} %collective-permute-done.8.refs_2_, ...), custom_call_target="tpu_custom_call" | custom-call | flops 536870912 | bytes 2621440 | tf_op jit(solution)/shard_map/weight_partials/pallas_call | solution.py:124
  115.8 31.9 %all_to_all.5 = bf16[64,16,256]{2,1,0:T(8,128)(2,1)S(1)} all-to-all(bf16[64,16,256]{2,1,0:T(8,128)(2,1)S(1)} %bitcast.25), channel_id=1, replica_groups=mesh['x_lo'=2,'z'=8,'core'=2,'y'=8,'x_hi'=2] {'z','y'}, dimensions={0} | all-to-all | bytes 1048576 | tf_op jit(solution)/shard_map/all_to_all | solution.py:240
  147.7 0.1 convert_reduce_fusion
  147.8 0.6 multiply_convert_fusion
  (2 shorter events, 0.0 us)
Async XLA Ops:
  1.4 11.3 %collective-permute-start = (bf16[128,256]{1,0:T(8,128)(2,1)S(1)}, bf16[128,256]{1,0:T(8,128)(2,1)S(1)}, u32[]{:S(2)}, u32[]{:S(2)}) collective-permute-start(bf16[128,256]{1,0:T(8,128)(2,1)S(1)} %pad_maximum_fusion.5), channel_id=1, source_target_pairs={{0,1},{1,0},{2,3},{3,2},{4,5},{5,4},{6,7},{7,6},{8,9},{9,8},{10,11... | collective-permute-start | bytes 196616 | tf_op jit(solution)/shard_map/ppermute | solution.py:148
  9.6 3.2 %copy-start.3 = (bf16[1,128,128]{2,1,0:T(8,128)(2,1)S(1)}, bf16[1,128,128]{2,1,0:T(8,128)(2,1)}, u32[]{:S(2)}) copy-start(bf16[1,128,128]{2,1,0:T(8,128)(2,1)} %param.10) | copy-start | bytes 98308
  9.6 3.2 %copy-start.4 = (bf16[1,128,128]{2,1,0:T(8,128)(2,1)S(1)}, bf16[1,128,128]{2,1,0:T(8,128)(2,1)}, u32[]{:S(2)}) copy-start(bf16[1,128,128]{2,1,0:T(8,128)(2,1)} %param.9) | copy-start | bytes 98308
  9.6 25.3 %copy-start = (bf16[1,128,1024]{2,1,0:T(8,128)(2,1)S(1)}, bf16[1,128,1024]{2,1,0:T(8,128)(2,1)}, u32[]{:S(2)}) copy-start(bf16[1,128,1024]{2,1,0:T(8,128)(2,1)} %param.8) | copy-start | bytes 786436
  9.6 25.3 %copy-start.1 = (bf16[1,128,1024]{2,1,0:T(8,128)(2,1)S(1)}, bf16[1,128,1024]{2,1,0:T(8,128)(2,1)}, u32[]{:S(2)}) copy-start(bf16[1,128,1024]{2,1,0:T(8,128)(2,1)} %param.11) | copy-start | bytes 786436
  9.6 25.3 %copy-start.2 = (s32[1,2048]{1,0:T(1,128)S(1)}, s32[1,2048]{1,0:T(1,128)}, u32[]{:S(2)}) copy-start(s32[1,2048]{1,0:T(1,128)} %refs_2_.1) | copy-start | bytes 24580
  10.8 67.5 %collective-permute-start.6 = (bf16[4096,128]{1,0:T(8,128)(2,1)}, bf16[4096,128]{1,0:T(8,128)(2,1)}, u32[]{:S(2)}, u32[]{:S(2)}) collective-permute-start(bf16[4096,128]{1,0:T(8,128)(2,1)} %bitcast.15), channel_id=1, source_target_pairs={{0,16},{16,0},{1,17},{17,1},{2,18},{18,2},{3,19},{19,3},{4,20},{20... | collective-permute-start | bytes 3145736 | tf_op jit(solution)/shard_map/ppermute | solution.py:148
  12.8 13.3 %collective-permute-start.4 = (bf16[256,256]{1,0:T(8,128)(2,1)S(1)}, bf16[256,256]{1,0:T(8,128)(2,1)S(1)}, u32[]{:S(2)}, u32[]{:S(2)}) collective-permute-start(bf16[256,256]{1,0:T(8,128)(2,1)S(1)} %pad_maximum_fusion.4.refs_5_), channel_id=1, source_target_pairs={{0,12},{2,14},{4,0},{6,2},{1,13},{3,15},{5,1},{7,3},{16,28},{18,30... | collective-permute-start | bytes 393224 | tf_op jit(solution)/shard_map/ppermute | solution.py:189
  18.1 13.5 %collective-permute-start.3 = (bf16[256,256]{1,0:T(8,128)(2,1)S(1)}, bf16[256,256]{1,0:T(8,128)(2,1)S(1)}, u32[]{:S(2)}, u32[]{:S(2)}) collective-permute-start(bf16[256,256]{1,0:T(8,128)(2,1)S(1)} %pad_maximum_fusion.4.refs_5_), channel_id=1, source_target_pairs={{0,6},{2,8},{4,10},{6,12},{8,14},{1,7},{3,9},{5,11},{7,13},{9,15},... | collective-permute-start | bytes 393224 | tf_op jit(solution)/shard_map/ppermute | solution.py:144
  20.2 11.9 %collective-permute-start.2 = (bf16[256,256]{1,0:T(8,128)(2,1)S(1)}, bf16[256,256]{1,0:T(8,128)(2,1)S(1)}, u32[]{:S(2)}, u32[]{:S(2)}) collective-permute-start(bf16[256,256]{1,0:T(8,128)(2,1)S(1)} %pad_maximum_fusion.4.refs_5_), channel_id=1, source_target_pairs={{0,4},{2,6},{4,8},{6,10},{8,12},{10,14},{1,5},{3,7},{5,9},{7,11},{... | collective-permute-start | bytes 393224 | tf_op jit(solution)/shard_map/ppermute | solution.py:144
  23.6 11.4 %collective-permute-start.1 = (bf16[256,256]{1,0:T(8,128)(2,1)S(1)}, bf16[256,256]{1,0:T(8,128)(2,1)S(1)}, u32[]{:S(2)}, u32[]{:S(2)}) collective-permute-start(bf16[256,256]{1,0:T(8,128)(2,1)S(1)} %pad_maximum_fusion.4.refs_5_), channel_id=1, source_target_pairs={{0,2},{2,4},{4,6},{6,8},{8,10},{10,12},{12,14},{1,3},{3,5},{5,7},{... | collective-permute-start | bytes 393224 | tf_op jit(solution)/shard_map/ppermute | solution.py:144
  26.2 8.8 %collective-permute-start.5 = (bf16[256,256]{1,0:T(8,128)(2,1)S(1)}, bf16[256,256]{1,0:T(8,128)(2,1)S(1)}, u32[]{:S(2)}, u32[]{:S(2)}) collective-permute-start(bf16[256,256]{1,0:T(8,128)(2,1)S(1)} %collective-permute-done.4), channel_id=1, source_target_pairs={{12,8},{14,10},{0,12},{2,14},{13,9},{15,11},{1,13},{3,15},{28,24},... | collective-permute-start | bytes 393224 | tf_op jit(solution)/shard_map/ppermute | solution.py:190
  41.9 9.6 %collective-permute-start.10 = (bf16[256,256]{1,0:T(8,128)(2,1)S(1)}, bf16[256,256]{1,0:T(8,128)(2,1)S(1)}, u32[]{:S(2)}, u32[]{:S(2)}) collective-permute-start(bf16[256,256]{1,0:T(8,128)(2,1)S(1)} %get-tuple-element.10), channel_id=1, source_target_pairs={{2,0},{4,2},{6,4},{8,6},{10,8},{12,10},{14,12},{3,1},{5,3},{7,5},{... | collective-permute-start | bytes 393224 | tf_op jit(solution)/shard_map/ppermute | solution.py:144
  45.7 12.5 %collective-permute-start.11 = (bf16[256,256]{1,0:T(8,128)(2,1)S(1)}, bf16[256,256]{1,0:T(8,128)(2,1)S(1)}, u32[]{:S(2)}, u32[]{:S(2)}) collective-permute-start(bf16[256,256]{1,0:T(8,128)(2,1)S(1)} %get-tuple-element.11), channel_id=1, source_target_pairs={{4,0},{6,2},{8,4},{10,6},{12,8},{14,10},{5,1},{7,3},{9,5},{11,7},{... | collective-permute-start | bytes 393224 | tf_op jit(solution)/shard_map/ppermute | solution.py:144
  47.0 19.5 %collective-permute-start.12 = (bf16[256,256]{1,0:T(8,128)(2,1)S(1)}, bf16[256,256]{1,0:T(8,128)(2,1)S(1)}, u32[]{:S(2)}, u32[]{:S(2)}) collective-permute-start(bf16[256,256]{1,0:T(8,128)(2,1)S(1)} %get-tuple-element.12), channel_id=1, source_target_pairs={{6,0},{8,2},{10,4},{12,6},{14,8},{7,1},{9,3},{11,5},{13,7},{15,9},... | collective-permute-start | bytes 393224 | tf_op jit(solution)/shard_map/ppermute | solution.py:144
  48.3 27.2 %collective-permute-start.13 = (bf16[256,256]{1,0:T(8,128)(2,1)S(1)}, bf16[256,256]{1,0:T(8,128)(2,1)S(1)}, u32[]{:S(2)}, u32[]{:S(2)}) collective-permute-start(bf16[256,256]{1,0:T(8,128)(2,1)S(1)} %get-tuple-element.13), channel_id=1, source_target_pairs={{8,0},{10,2},{12,4},{14,6},{9,1},{11,3},{13,5},{15,7},{24,16},{26,... | collective-permute-start | bytes 393224 | tf_op jit(solution)/shard_map/ppermute | solution.py:144
  75.6 15.0 %collective-permute-start.14 = (bf16[256,256]{1,0:T(8,128)(2,1)S(1)}, bf16[256,256]{1,0:T(8,128)(2,1)S(1)}, u32[]{:S(2)}, u32[]{:S(2)}) collective-permute-start(bf16[256,256]{1,0:T(8,128)(2,1)S(1)} %fusion), channel_id=1, source_target_pairs={{0,1},{1,0},{2,3},{3,2},{4,5},{5,4},{6,7},{7,6},{8,9},{9,8},{10,11... | collective-permute-start | bytes 393224 | tf_op jit(solution)/shard_map/ppermute | solution.py:148
  79.8 34.1 %collective-permute-start.7 = (bf16[1024,256]{1,0:T(8,128)(2,1)S(1)}, bf16[1024,256]{1,0:T(8,128)(2,1)S(1)}, u32[]{:S(2)}, u32[]{:S(2)}) collective-permute-start(bf16[1024,256]{1,0:T(8,128)(2,1)S(1)} %pad_maximum_fusion.1), channel_id=1, source_target_pairs={{0,1},{1,0},{256,257},{257,256},{2,3},{3,2},{258,259},{259,258},{4... | collective-permute-start | bytes 1572872 | tf_op jit(solution)/shard_map/ppermute | solution.py:153
  84.5 29.4 %collective-permute-start.8 = (bf16[1024,256]{1,0:T(8,128)(2,1)S(1)}, bf16[1024,256]{1,0:T(8,128)(2,1)S(1)}, u32[]{:S(2)}, u32[]{:S(2)}) collective-permute-start(bf16[1024,256]{1,0:T(8,128)(2,1)S(1)} %pad_maximum_fusion.2), channel_id=1, source_target_pairs={{0,256},{1,257},{256,0},{257,1},{2,258},{3,259},{258,2},{259,3},{4... | collective-permute-start | bytes 1572872 | tf_op jit(solution)/shard_map/ppermute | solution.py:153
  87.9 26.1 %collective-permute-start.9 = (bf16[1024,256]{1,0:T(8,128)(2,1)}, bf16[1024,256]{1,0:T(8,128)(2,1)S(1)}, u32[]{:S(2)}, u32[]{:S(2)}) collective-permute-start(bf16[1024,256]{1,0:T(8,128)(2,1)} %pad_maximum_fusion.3), channel_id=1, source_target_pairs={{0,257},{1,256},{256,1},{257,0},{2,259},{3,258},{258,3},{259,2},{4... | collective-permute-start | bytes 1572872 | tf_op jit(solution)/shard_map/ppermute | solution.py:153
  90.7 19.5 %collective-permute-start.17 = (bf16[256,256]{1,0:T(8,128)(2,1)S(1)}, bf16[256,256]{1,0:T(8,128)(2,1)S(1)}, u32[]{:S(2)}, u32[]{:S(2)}) collective-permute-start(bf16[256,256]{1,0:T(8,128)(2,1)S(1)} %add_convert_fusion.refs_4_), channel_id=1, source_target_pairs={{0,272},{16,256},{256,16},{272,0},{1,273},{17,257},{257,17},{273,1... | collective-permute-start | bytes 393224 | tf_op jit(solution)/shard_map/ppermute | solution.py:234
  92.6 20.5 %collective-permute-start.16 = (bf16[256,256]{1,0:T(8,128)(2,1)S(1)}, bf16[256,256]{1,0:T(8,128)(2,1)S(1)}, u32[]{:S(2)}, u32[]{:S(2)}) collective-permute-start(bf16[256,256]{1,0:T(8,128)(2,1)S(1)} %add_convert_fusion.refs_4_), channel_id=1, source_target_pairs={{0,256},{256,0},{1,257},{257,1},{2,258},{258,2},{3,259},{259,3},{4... | collective-permute-start | bytes 393224 | tf_op jit(solution)/shard_map/ppermute | solution.py:234
  110.2 3.7 %collective-permute-start.15 = (bf16[256,256]{1,0:T(8,128)(2,1)S(1)}, bf16[256,256]{1,0:T(8,128)(2,1)S(1)}, u32[]{:S(2)}, u32[]{:S(2)}) collective-permute-start(bf16[256,256]{1,0:T(8,128)(2,1)S(1)} %add_convert_fusion.refs_4_), channel_id=1, source_target_pairs={{0,16},{16,0},{1,17},{17,1},{2,18},{18,2},{3,19},{19,3},{4,20},{20... | collective-permute-start | bytes 393224 | tf_op jit(solution)/shard_map/ppermute | solution.py:234
